TPU v7x, 256 devices: a whole 4x4x8 slice. The times are simulated.
256 devices in a mesh: gz: 128 (over x, y, z), gx: 2 (over core).
Axes of the slice: x: 4, y: 4, z: 8, core: 2. Of those that a mesh axis runs over, the one named last changes fastest.
Arguments:
- b_field: float32 [3, 48, 1024, 256], P(None, 'gx', 'gz'), may hold values from -6 to 6
- resist: float32 [48, 1024, 256], P('gx', 'gz'), may hold values from 0.05 to 0.8
- ymix: float32 [256, 256], replicated, may hold values from -0.5 to 1.5
- zmix: float32 [1024, 1024], replicated, may hold values from -0.5 to 1.5
Outputs:
- b_next: float32 [3, 48, 1024, 256], P(None, 'gx', 'gz')
- potential: float32 [3, 48, 1024, 256], P(None, 'gx', 'gz')
All inputs are finite; a program needn't handle non-finite values.
Results may differ from a plain program's by a relative error of at most 0.000073.
Values sent between devices are 32-bit elements; how exact they have to be, the bound alone decides.
A program may use at most 64 MiB of HBM per device.

v0:
```python
import functools

import jax
import jax.numpy as jnp
from jax import lax
from jax.experimental import pallas as pl
from jax.experimental.pallas import tpu as pltpu
from jax.sharding import PartitionSpec as P

MESH = pl.DeviceIdType.MESH
F32, BF16 = jnp.float32, jnp.bfloat16
TIME_STEP = 0.1
NX, NZL, NY = 24, 8, 256
LINES = 3 * NX
SLABS = 128
XR = 32


def split(value):
    high = value.astype(BF16)
    return high, (value - high.astype(F32)).astype(BF16)


def dot(lhs, rhs, rhs_dim=0):
    return lax.dot_general(
        lhs, rhs, (((1,), (rhs_dim,)), ((), ())), preferred_element_type=F32
    )


def dot3(lhs, rhs, rhs_dim=0):
    (lhs_hi, lhs_lo), (rhs_hi, rhs_lo) = lhs, rhs
    small = dot(lhs_lo, rhs_hi, rhs_dim) + dot(lhs_hi, rhs_lo, rhs_dim)
    return small + dot(lhs_hi, rhs_hi, rhs_dim)


def diff(value, axis):
    size = value.shape[axis]
    return pltpu.roll(value, size - 1, axis) - pltpu.roll(value, 1, axis)


def halo_copies(b, res, bp, send, recv):
    gz, gx = lax.axis_index("gz"), lax.axis_index("gx")
    down, up = lax.rem(gz + SLABS - 1, SLABS), lax.rem(gz + 1, SLABS)
    other = 1 - gx
    near, far = (NX - 1) * other, gx + (NX - 2) * other
    near_row, far_row = 24 + 7 * other, 25 + 5 * other
    rows = slice(0, NX)
    same, cross = lambda z: {"gz": z}, lambda z: {"gz": z, "gx": other}
    plan = (
        (b.at[:, :, 0], bp.at[0:3, 10, rows], same(down)),
        (b.at[:, :, 7], bp.at[0:3, 1, rows], same(up)),
        (b.at[0:2, :, 1], bp.at[0:2, 11, rows], same(down)),
        (b.at[0:2, :, 6], bp.at[0:2, 0, rows], same(up)),
        (res.at[:, 0], bp.at[3, 10, rows], same(down)),
        (res.at[:, 7], bp.at[3, 1, rows], same(up)),
        (b.at[:, near], bp.at[0:3, 2:10, near_row], cross(gz)),
        (b.at[1:3, far], bp.at[1:3, 2:10, far_row], cross(gz)),
        (res.at[near], bp.at[3, 2:10, near_row], cross(gz)),
        (b.at[:, near, 0], bp.at[0:3, 10, near_row], cross(down)),
        (b.at[:, near, 7], bp.at[0:3, 1, near_row], cross(up)),
    )
    return [
        pltpu.make_async_remote_copy(
            src_ref=src,
            dst_ref=dst,
            send_sem=send.at[i],
            recv_sem=recv.at[i],
            device_id=where,
            device_id_type=MESH,
        )
        for i, (src, dst, where) in enumerate(plan)
    ]


def exchange(src, dst, send, recv, own):
    me = lax.axis_index("gz")
    pltpu.make_async_copy(src.at[:, me], dst.at[:, me], own).start()

    @pl.loop(1, SLABS)
    def _(step):
        peer = lax.rem(me + step, SLABS)
        pltpu.make_async_remote_copy(
            src_ref=src.at[:, peer],
            dst_ref=dst.at[:, me],
            send_sem=send,
            recv_sem=recv,
            device_id={"gz": peer},
            device_id_type=MESH,
        ).start()


def exchange_wait(src, dst, send, recv, own):
    rest = pl.ds(0, SLABS - 1)
    pltpu.make_async_copy(src.at[:, 0], dst.at[:, 0], own).wait()
    pltpu.make_async_copy(dst.at[:, rest], dst.at[:, rest], recv).wait()


def exchange_sent(src, send):
    rest = pl.ds(0, SLABS - 1)
    pltpu.make_async_copy(src.at[:, rest], src.at[:, rest], send).wait()


def electric_plane(bp, ef, p):
    bx, by, bz, rs = bp[0, p], bp[1, p], bp[2, p], bp[3, p]
    jx = (diff(bz, 1) - (bp[1, p + 1] - bp[1, p - 1])) * 0.5
    jy = ((bp[0, p + 1] - bp[0, p - 1]) - diff(bz, 0)) * 0.5
    jz = (diff(by, 0) - diff(bx, 1)) * 0.5
    square = bx * bx + by * by + bz * bz
    inverse = 1.0 / (square + 1.0)
    along = (jx * bx + jy * by + jz * bz) * inverse
    factor = rs + square * inverse
    ef[0, p - 1] = jx * factor - bx * along
    ef[1, p - 1] = jy * factor - by * along
    ef[2, p - 1] = jz * factor - bz * along


def stepped_plane(bp, ef, st, r):
    ex, ey, ez = ef[0, r + 1], ef[1, r + 1], ef[2, r + 1]
    half = 0.5 * TIME_STEP
    cx = diff(ez, 1) - (ef[1, r + 2] - ef[1, r])
    cy = (ef[0, r + 2] - ef[0, r]) - diff(ez, 0)
    cz = diff(ey, 0) - diff(ex, 1)
    for c, curl in enumerate((cx, cy, cz)):
        row = pl.multiple_of(LINES + r * LINES + c * NX, 8)
        st[pl.ds(row, NX), :] = (bp[c, r + 2] - half * curl)[0:NX]


def kernel(
    b, res, ymix, zmix, next_ref, pot_ref,
    bp, ef, st, yv, zv, zt, zhi, zlo, rhi, rlo, fsend, frecv, osend, orecv, o1, o2,
    hs, hr, s1, r1, s2, r2, own, loads,
):
    gz, gx = lax.axis_index("gz"), lax.axis_index("gx")
    load_b = [pltpu.make_async_copy(b.at[:, :, z], bp.at[0:3, z + 2, 0:NX], loads.at[0]) for z in range(NZL)]
    load_r = [pltpu.make_async_copy(res.at[:, z], bp.at[3, z + 2, 0:NX], loads.at[1]) for z in range(NZL)]
    load_y = pltpu.make_async_copy(ymix, yv, loads.at[2])
    load_z = [pltpu.make_async_copy(zmix.at[:, k * 128 : (k + 1) * 128], zv.at[k], loads.at[3]) for k in range(8)]
    for copy in (*load_b, *load_r, load_y, *load_z):
        copy.start()
    bp[:, :, NX:XR, :] = jnp.zeros((4, 12, XR - NX, NY), F32)

    barrier = pltpu.get_barrier_semaphore()
    other = 1 - gx
    down, up = lax.rem(gz + SLABS - 1, SLABS), lax.rem(gz + 1, SLABS)
    for z in (down, gz, up):
        pl.semaphore_signal(barrier, inc=1, device_id={"gz": z, "gx": other}, device_id_type=MESH)

    @pl.loop(1, SLABS)
    def _(step):
        peer = lax.rem(gz + step, SLABS)
        pl.semaphore_signal(barrier, inc=1, device_id={"gz": peer}, device_id_type=MESH)

    pl.semaphore_wait(barrier, SLABS + 2)
    halo = halo_copies(b, res, bp, hs, hr)
    for copy in halo:
        copy.start()

    st[0:LINES, :] = jnp.zeros((LINES, NY), F32)
    st[9 * LINES :, :] = jnp.zeros((st.shape[0] - 9 * LINES, NY), F32)
    load_y.wait()
    y_hi, y_lo = split(yv[...].T)
    pltpu.make_async_copy(bp.at[0:3, 2:10, 0:NX], bp.at[0:3, 2:10, 0:NX], loads.at[0]).wait()
    pltpu.make_async_copy(bp.at[3, 2:10, 0:NX], bp.at[3, 2:10, 0:NX], loads.at[1]).wait()
    for copy in halo:
        copy.wait()

    @pl.when(gz == 0)
    def _():
        bp[:, 0:2] = jnp.zeros((4, 2, XR, NY), F32)

    @pl.when(gz == SLABS - 1)
    def _():
        bp[:, 10:12] = jnp.zeros((4, 2, XR, NY), F32)

    @pl.loop(1, 11)
    def _(p):
        electric_plane(bp, ef, p)

    @pl.loop(0, NZL)
    def _(r):
        stepped_plane(bp, ef, st, r)

    lane = lax.broadcasted_iota(jnp.int32, (SLABS, 128), 1)
    below = None
    for q in range(NZL + 1):
        mixed = dot3((y_hi, y_lo), split(st[q * LINES : q * LINES + 128, :]), 1)
        if q:
            fsend[q - 1] = jnp.where(lane < LINES, mixed[0:128], below)
        below = mixed[128:256]
    ends = jnp.concatenate([st[r * LINES + 128 : r * LINES + 144, :] for r in range(NZL)], axis=0)
    fsend[NZL] = dot3((y_hi[128:256], y_lo[128:256]), split(ends), 1)
    exchange(fsend, frecv, s1, r1, own.at[0])

    pltpu.make_async_copy(zv, zv, loads.at[3]).wait()
    row_id = lax.broadcasted_iota(jnp.int32, (SLABS, SLABS), 0)
    col_id = lax.broadcasted_iota(jnp.int32, (SLABS, SLABS), 1)
    lower = (col_id < row_id).astype(F32)

    @pl.loop(0, NZL)
    def _(r):
        for k in range(8):
            zt[k * 128 : (k + 1) * 128, :] = zv[k, pl.ds(r, SLABS, stride=8), :].T
        column = pl.ds(pl.multiple_of(r * SLABS, SLABS), SLABS)
        total = jnp.zeros((SLABS, SLABS), F32)
        for k in range(8):
            part = zt[pl.ds(k, SLABS, stride=8), :]
            total = total + part
            zhi[k * 128 : (k + 1) * 128, column], zlo[k * 128 : (k + 1) * 128, column] = split(part)
        under = lax.dot_general(
            lower, total, (((1,), (0,)), ((), ())),
            precision=lax.Precision.HIGHEST, preferred_element_type=F32,
        )
        zhi[1024:1152, column], zlo[1024:1152, column] = split(under)

    exchange_wait(fsend, frecv, s1, r1, own.at[0])
    tail = frecv[NZL]
    for r in range(NZL):
        rows = slice(r * SLABS, (r + 1) * SLABS)
        rhi[rows, 0:128], rlo[rows, 0:128] = split(frecv[r])
        moved = pltpu.roll(tail, (128 - 16 * r) % 128, 1) if r else tail
        rhi[rows, 128:256], rlo[rows, 128:256] = split(moved)

    packed = jnp.zeros((SLABS, 128), F32)
    for k in range(9):
        rows = slice(k * SLABS, (k + 1) * SLABS)
        mixed = dot3((zhi[rows, :], zlo[rows, :]), (rhi[...], rlo[...]))
        osend[k] = mixed[:, 0:128]
        end = mixed[:, 128:256]
        if k < 8:
            moved = pltpu.roll(end, 16 * k, 1) if k else end
            packed = jnp.where((lane >= 16 * k) & (lane < 16 * k + 16), moved, packed)
        else:
            osend[10] = end
    osend[9] = packed
    exchange(osend, orecv, s2, r2, own.at[1])
    exchange_sent(fsend, s1)
    exchange_wait(osend, orecv, s2, r2, own.at[1])

    scale = float(NZL * SLABS) ** -0.5
    column = orecv[8].T
    end_column = orecv[10].T[0:16]
    ends = orecv[9].T
    pieces = (
        (0, 24, 0, 192, -1.0, 0), (24, 48, 192, 0, 1.0, 0), (48, 72, 384, 384, 1.0, 0),
        (72, 96, 0, 192, -1.0, 1), (96, 120, 192, 0, 1.0, 1), (120, 128, 384, 384, 1.0, 1),
    )
    for k in range(NZL):
        lines = orecv[k].T
        column = column + lines
        for first, last, at, to, sign, half in pieces:
            o1[half, pl.ds(at + k, last - first, stride=8), :] = lines[first:last]
            o2[half, pl.ds(to + k, last - first, stride=8), :] = column[first:last] * (sign * scale)
        end = ends[16 * k : 16 * k + 16]
        end_column = end_column + end
        o1[1, pl.ds(448 + k, 16, stride=8), :] = end
        o2[1, pl.ds(448 + k, 16, stride=8), :] = end_column * scale
    out = [
        pltpu.make_async_copy(src.at[half], dst.at[:, half * 128 : half * 128 + 128], loads.at[4 + 2 * i + half])
        for i, (src, dst) in enumerate(((o1, next_ref), (o2, pot_ref)))
        for half in range(2)
    ]
    for copy in out:
        copy.start()
    exchange_sent(osend, s2)
    for copy in out:
        copy.wait()


def on_device(b_field, resist, ymix, zmix):
    flat = (3 * NX * NZL, NY)
    dma = pltpu.SemaphoreType.DMA
    b_next, potential = pl.pallas_call(
        kernel,
        name="step",
        out_shape=(jax.ShapeDtypeStruct(flat, F32), jax.ShapeDtypeStruct(flat, F32)),
        in_specs=[pl.BlockSpec(memory_space=pl.ANY)] * 4,
        out_specs=[pl.BlockSpec(memory_space=pl.ANY)] * 2,
        scratch_shapes=[
            pltpu.VMEM((4, NZL + 4, XR, NY), F32),
            pltpu.VMEM((3, NZL + 2, XR, NY), F32),
            pltpu.VMEM((LINES * 10, NY), F32),
            pltpu.VMEM((NY, NY), F32),
            pltpu.VMEM((8, 1024, 128), F32),
            pltpu.VMEM((1024, 128), F32),
            pltpu.VMEM((1152, 1024), BF16),
            pltpu.VMEM((1152, 1024), BF16),
            pltpu.VMEM((1024, 256), BF16),
            pltpu.VMEM((1024, 256), BF16),
            pltpu.VMEM((9, SLABS, 128), F32),
            pltpu.VMEM((9, SLABS, 128), F32),
            pltpu.VMEM((11, SLABS, 128), F32),
            pltpu.VMEM((11, SLABS, 128), F32),
            pltpu.VMEM((2, flat[0], 128), F32),
            pltpu.VMEM((2, flat[0], 128), F32),
            dma((11,)), dma((11,)), dma(()), dma(()), dma(()), dma(()), dma((2,)), dma((8,)),
        ],
        compiler_params=pltpu.CompilerParams(
            collective_id=0, has_side_effects=True, vmem_limit_bytes=50 * 2**20
        ),
    )(b_field, resist, ymix, zmix)
    return b_next.reshape(b_field.shape), potential.reshape(b_field.shape)


def solution(mesh):
    in_specs = (P(None, "gx", "gz", None), P("gx", "gz", None), P(), P())
    out_specs = (P(None, "gx", "gz", None), P(None, "gx", "gz", None))
    return jax.shard_map(
        on_device, mesh=mesh, in_specs=in_specs, out_specs=out_specs, check_vma=False
    )
```

profile of v0, /device:TPU:8, one launch (start us, length us, event | category | flops | bytes accessed | tf_op | source)
XLA Modules:
  0.0 66.3 jit_solution(8104199569539422729)
XLA Ops:
  0.6 0.0 copy-start
  0.6 1.1 %copy-done = f32[3,24,8,256]{3,2,1,0:T(8,128)S(1)} copy-done((f32[3,24,8,256]{3,2,1,0:T(8,128)S(1)}, f32[3,24,8,256]{3,2,1,0:T(8,128)}, u32[]{:S(2)}) %copy-start) | copy-done | bytes 589848
  1.7 0.0 copy-start.1
  1.7 0.9 %copy-done.1 = f32[256,256]{1,0:T(8,128)S(1)} copy-done((f32[256,256]{1,0:T(8,128)S(1)}, f32[256,256]{1,0:T(8,128)}, u32[]{:S(2)}) %copy-start.1) | copy-done | bytes 262168
  2.6 0.0 copy-start.2
  2.6 0.9 %copy-done.2 = f32[24,8,256]{2,1,0:T(8,128)S(1)} copy-done((f32[24,8,256]{2,1,0:T(8,128)S(1)}, f32[24,8,256]{2,1,0:T(8,128)}, u32[]{:S(2)}) %copy-start.2) | copy-done | bytes 196632
  3.6 61.0 %step.1 = (f32[576,256]{1,0:T(8,128)S(1)}, f32[576,256]{1,0:T(8,128)S(1)}) custom-call(f32[3,24,8,256]{3,2,1,0:T(8,128)S(1)} %copy-done, f32[24,8,256]{2,1,0:T(8,128)S(1)} %copy-done.2, f32[256,256]{1,0:T(8,128)S(1)} %copy-done.1, f32[1024,1024]{1,0:T(8,128)} %zmix.1), custom_call_target="tpu_custom_call" | custom-call | tf_op jit(solution)/shard_map/step/pallas_call | solution.py:272
  64.6 0.8 %copy.8 = f32[3,24,8,256]{3,2,1,0:T(8,128)} copy(f32[3,24,8,256]{3,2,1,0:T(8,128)S(1)} %bitcast.3) | data formatting | bytes 1179648
  65.4 0.8 %copy.9 = f32[3,24,8,256]{3,2,1,0:T(8,128)} copy(f32[3,24,8,256]{3,2,1,0:T(8,128)S(1)} %bitcast.2) | data formatting | bytes 1179648
Async XLA Ops:
  0.6 1.1 %copy-start = (f32[3,24,8,256]{3,2,1,0:T(8,128)S(1)}, f32[3,24,8,256]{3,2,1,0:T(8,128)}, u32[]{:S(2)}) copy-start(f32[3,24,8,256]{3,2,1,0:T(8,128)} %b.1) | copy-start | bytes 1769476
  1.7 0.9 %copy-start.1 = (f32[256,256]{1,0:T(8,128)S(1)}, f32[256,256]{1,0:T(8,128)}, u32[]{:S(2)}) copy-start(f32[256,256]{1,0:T(8,128)} %ymix.1) | copy-start | bytes 786436
  2.6 0.9 %copy-start.2 = (f32[24,8,256]{2,1,0:T(8,128)S(1)}, f32[24,8,256]{2,1,0:T(8,128)}, u32[]{:S(2)}) copy-start(f32[24,8,256]{2,1,0:T(8,128)} %res.1) | copy-start | bytes 589828
where the time goes:
time: 66.4 us; the launch traced here: 66.3 us
  Pallas kernels  61 us (92%)
  local copies, waits for them, and re-layouts  4.56 us (7%)
    pallas_call x1, Pallas kernels, on_device(): pl.pallas_call(kernel, name='step', out_shape=(jax.ShapeDtypeStruct(flat,...  61 us
    unnamed x8, local copies, waits for them, and re-layouts  4.56 us

commit v1 on v0

v1 whole, which is shorter than its diff:
```python
import functools

import jax
import jax.numpy as jnp
from jax import lax
from jax.experimental import pallas as pl
from jax.experimental.pallas import tpu as pltpu
from jax.sharding import PartitionSpec as P

MESH = pl.DeviceIdType.MESH
F32, BF16 = jnp.float32, jnp.bfloat16
TIME_STEP = 0.1
NX, NZL, NY = 24, 8, 256
LINES = 3 * NX
SLABS = 128
XR = 32


def split(value):
    high = value.astype(BF16)
    return high, (value - high.astype(F32)).astype(BF16)


def dot(lhs, rhs, rhs_dim=0):
    return lax.dot_general(
        lhs, rhs, (((1,), (rhs_dim,)), ((), ())), preferred_element_type=F32
    )


def dot3(lhs, rhs, rhs_dim=0):
    (lhs_hi, lhs_lo), (rhs_hi, rhs_lo) = lhs, rhs
    small = dot(lhs_lo, rhs_hi, rhs_dim) + dot(lhs_hi, rhs_lo, rhs_dim)
    return small + dot(lhs_hi, rhs_hi, rhs_dim)


def diff(value, axis):
    size = value.shape[axis]
    return pltpu.roll(value, size - 1, axis) - pltpu.roll(value, 1, axis)


def halo_copies(b, res, bp, send, recv):
    gz, gx = lax.axis_index("gz"), lax.axis_index("gx")
    down, up = lax.rem(gz + SLABS - 1, SLABS), lax.rem(gz + 1, SLABS)
    other = 1 - gx
    near, far = (NX - 1) * other, gx + (NX - 2) * other
    near_row, far_row = 24 + 7 * other, 25 + 5 * other
    rows = slice(0, NX)
    same, cross = lambda z: {"gz": z}, lambda z: {"gz": z, "gx": other}
    plan = (
        (b.at[:, near], bp.at[0:3, 2:10, near_row], cross(gz)),
        (b.at[1:3, far], bp.at[1:3, 2:10, far_row], cross(gz)),
        (res.at[near], bp.at[3, 2:10, near_row], cross(gz)),
        (b.at[:, :, 0], bp.at[0:3, 10, rows], same(down)),
        (b.at[:, :, 7], bp.at[0:3, 1, rows], same(up)),
        (b.at[0:2, :, 1], bp.at[0:2, 11, rows], same(down)),
        (b.at[0:2, :, 6], bp.at[0:2, 0, rows], same(up)),
        (res.at[:, 0], bp.at[3, 10, rows], same(down)),
        (res.at[:, 7], bp.at[3, 1, rows], same(up)),
        (b.at[:, near, 0], bp.at[0:3, 10, near_row], cross(down)),
        (b.at[:, near, 7], bp.at[0:3, 1, near_row], cross(up)),
    )
    return [
        pltpu.make_async_remote_copy(
            src_ref=src,
            dst_ref=dst,
            send_sem=send.at[i],
            recv_sem=recv.at[i],
            device_id=where,
            device_id_type=MESH,
        )
        for i, (src, dst, where) in enumerate(plan)
    ]


def exchange(src, dst, first, last, send, recv, own):
    me = lax.axis_index("gz")
    if src.ndim == 2:
        part, every = lambda ref, d: ref.at[d], lambda ref: ref.at[0 : SLABS - 1]
    else:
        part, every = lambda ref, d: ref.at[first:last, d], lambda ref: ref.at[first:last, 0 : SLABS - 1]
    here = pltpu.make_async_copy(part(src, me), part(dst, me), own)
    here.start()

    @pl.loop(1, SLABS)
    def _(step):
        peer = lax.rem(me + step, SLABS)
        pltpu.make_async_remote_copy(
            src_ref=part(src, peer),
            dst_ref=part(dst, me),
            send_sem=send,
            recv_sem=recv,
            device_id={"gz": peer},
            device_id_type=MESH,
        ).start()

    def arrived():
        here.wait()
        pltpu.make_async_copy(every(dst), every(dst), recv).wait()

    def sent():
        pltpu.make_async_copy(every(src), every(src), send).wait()

    return arrived, sent


def electric_plane(bp, ef, p):
    bx, by, bz, rs = bp[0, p], bp[1, p], bp[2, p], bp[3, p]
    jx = (diff(bz, 1) - (bp[1, p + 1] - bp[1, p - 1])) * 0.5
    jy = ((bp[0, p + 1] - bp[0, p - 1]) - diff(bz, 0)) * 0.5
    jz = (diff(by, 0) - diff(bx, 1)) * 0.5
    square = bx * bx + by * by + bz * bz
    inverse = 1.0 / (square + 1.0)
    along = (jx * bx + jy * by + jz * bz) * inverse
    factor = rs + square * inverse
    ef[0, p - 1] = jx * factor - bx * along
    ef[1, p - 1] = jy * factor - by * along
    ef[2, p - 1] = jz * factor - bz * along


def stepped_plane(bp, ef, st, r):
    ex, ey, ez = ef[0, r + 1], ef[1, r + 1], ef[2, r + 1]
    half = 0.5 * TIME_STEP
    cx = diff(ez, 1) - (ef[1, r + 2] - ef[1, r])
    cy = (ef[0, r + 2] - ef[0, r]) - diff(ez, 0)
    cz = diff(ey, 0) - diff(ex, 1)
    for c, curl in enumerate((cx, cy, cz)):
        row = pl.multiple_of(LINES + r * LINES + c * NX, 8)
        st[pl.ds(row, NX), :] = (bp[c, r + 2] - half * curl)[0:NX]


def mix_rows(st, rows, mixer, out, tails, first, half):
    lane = lax.broadcasted_iota(jnp.int32, (SLABS, 128), 1)
    high, low = mixer
    blocks = {}
    for q in sorted({*rows, *(r + 1 for r in rows)}):
        blocks[q] = dot3(mixer, split(st[q * LINES : q * LINES + 128, :]), 1)
    for i, r in enumerate(rows):
        out[first + i] = jnp.where(lane < LINES, blocks[r + 1][0:128], blocks[r][128:256])
    ends = jnp.concatenate([st[r * LINES + 128 : r * LINES + 144, :] for r in rows], axis=0)
    tails[half] = dot3((high[128:256], low[128:256]), split(ends), 1)


def prepare(zv, zt, zhi, zlo, first, last):
    row_id = lax.broadcasted_iota(jnp.int32, (SLABS, SLABS), 0)
    col_id = lax.broadcasted_iota(jnp.int32, (SLABS, SLABS), 1)
    lower = (col_id < row_id).astype(F32)

    @pl.loop(first, last)
    def _(slot):
        r = lax.rem(slot + 2, NZL)
        for k in range(8):
            zt[k * 128 : (k + 1) * 128, :] = zv[k, pl.ds(r, SLABS, stride=8), :].T
        column = pl.ds(pl.multiple_of(slot * SLABS, SLABS), SLABS)
        total = jnp.zeros((SLABS, SLABS), F32)
        for k in range(8):
            part = zt[pl.ds(k, SLABS, stride=8), :]
            total = total + part
            zhi[k * 128 : (k + 1) * 128, column], zlo[k * 128 : (k + 1) * 128, column] = split(part)
        under = lax.dot_general(
            lower, total, (((1,), (0,)), ((), ())),
            precision=lax.Precision.HIGHEST, preferred_element_type=F32,
        )
        zhi[1024:1152, column], zlo[1024:1152, column] = split(under)


def take_rows(frecv, trecv, rhi, rlo, half):
    zeros = jnp.zeros((SLABS, 64), F32)
    tail = jnp.concatenate([trecv[half], zeros], axis=1)
    for i in range(4):
        slot = 4 * half + i
        rows = slice(slot * SLABS, (slot + 1) * SLABS)
        rhi[rows, 0:128], rlo[rows, 0:128] = split(frecv[slot])
        moved = pltpu.roll(tail, 128 - 16 * i, 1) if i else tail
        rhi[rows, 128:256], rlo[rows, 128:256] = split(moved)


def kernel(
    b, res, ymix, zmix, next_ref, pot_ref,
    bp, ef, st, yv, zv, zt, zhi, zlo, rhi, rlo, acc,
    fsend, frecv, tsend, trecv, osend, orecv, esend, erecv, o1, o2,
    hs, hr, send, recv, own, loads,
):
    gz, gx = lax.axis_index("gz"), lax.axis_index("gx")
    load_b = [pltpu.make_async_copy(b.at[:, :, z], bp.at[0:3, z + 2, 0:NX], loads.at[0]) for z in range(NZL)]
    load_r = [pltpu.make_async_copy(res.at[:, z], bp.at[3, z + 2, 0:NX], loads.at[1]) for z in range(NZL)]
    load_y = pltpu.make_async_copy(ymix, yv, loads.at[2])
    load_z = [pltpu.make_async_copy(zmix.at[:, k * 128 : (k + 1) * 128], zv.at[k], loads.at[3]) for k in range(8)]
    for copy in (*load_b, *load_r, load_y, *load_z):
        copy.start()
    bp[:, :, NX:XR, :] = jnp.zeros((4, 12, XR - NX, NY), F32)

    barrier = pltpu.get_barrier_semaphore()
    other = 1 - gx
    down, up = lax.rem(gz + SLABS - 1, SLABS), lax.rem(gz + 1, SLABS)
    for z in (down, gz, up):
        pl.semaphore_signal(barrier, inc=1, device_id={"gz": z, "gx": other}, device_id_type=MESH)

    @pl.loop(1, SLABS)
    def _(step):
        peer = lax.rem(gz + step, SLABS)
        pl.semaphore_signal(barrier, inc=1, device_id={"gz": peer}, device_id_type=MESH)

    st[...] = jnp.zeros(st.shape, F32)
    load_y.wait()
    mixer = split(yv[...].T)
    pl.semaphore_wait(barrier, SLABS + 2)
    halo = halo_copies(b, res, bp, hs, hr)
    for copy in halo:
        copy.start()

    pltpu.make_async_copy(bp.at[0:3, 2:10, 0:NX], bp.at[0:3, 2:10, 0:NX], loads.at[0]).wait()
    pltpu.make_async_copy(bp.at[3, 2:10, 0:NX], bp.at[3, 2:10, 0:NX], loads.at[1]).wait()
    for copy in halo[:3]:
        copy.wait()

    @pl.loop(3, 9)
    def _(p):
        electric_plane(bp, ef, p)

    @pl.loop(2, 6)
    def _(r):
        stepped_plane(bp, ef, st, r)

    mix_rows(st, (2, 3, 4, 5), mixer, fsend, tsend, 0, 0)
    waits = [
        exchange(fsend, frecv, 0, 4, send.at[0], recv.at[0], own.at[0]),
        exchange(tsend, trecv, 0, 1, send.at[1], recv.at[1], own.at[1]),
    ]
    for copy in halo[3:]:
        copy.wait()

    @pl.when(gz == 0)
    def _():
        bp[:, 0:2] = jnp.zeros((4, 2, XR, NY), F32)

    @pl.when(gz == SLABS - 1)
    def _():
        bp[:, 10:12] = jnp.zeros((4, 2, XR, NY), F32)

    for p in (1, 2, 9, 10):
        electric_plane(bp, ef, p)
    for r in (0, 1, 6, 7):
        stepped_plane(bp, ef, st, r)
    mix_rows(st, (6, 7, 0, 1), mixer, fsend, tsend, 4, 1)
    waits += [
        exchange(fsend, frecv, 4, 8, send.at[2], recv.at[2], own.at[2]),
        exchange(tsend, trecv, 1, 2, send.at[3], recv.at[3], own.at[3]),
    ]
    pltpu.make_async_copy(zv, zv, loads.at[3]).wait()
    prepare(zv, zt, zhi, zlo, 0, NZL)

    waits[0][0]()
    waits[1][0]()
    take_rows(frecv, trecv, rhi, rlo, 0)
    for k in range(9):
        rows = slice(k * SLABS, (k + 1) * SLABS)
        acc[rows, :] = dot3((zhi[rows, 0:512], zlo[rows, 0:512]), (rhi[0:512, :], rlo[0:512, :]))
    waits[2][0]()
    waits[3][0]()
    take_rows(frecv, trecv, rhi, rlo, 1)

    lane = lax.broadcasted_iota(jnp.int32, (SLABS, 128), 1)
    packed = jnp.zeros((SLABS, 128), F32)
    groups = ((0, 3), (3, 6), (6, 10))
    for g, (first, last) in enumerate(groups):
        for slot in range(first, min(last, 9)):
            k = (slot + 8) % 9
            rows = slice(k * SLABS, (k + 1) * SLABS)
            mixed = acc[rows, :] + dot3(
                (zhi[rows, 512:1024], zlo[rows, 512:1024]), (rhi[512:1024, :], rlo[512:1024, :])
            )
            osend[slot] = mixed[:, 0:128]
            end = mixed[:, 128:256]
            if slot:
                moved = pltpu.roll(end, 16 * k, 1) if k else end
                packed = jnp.where((lane >= 16 * k) & (lane < 16 * k + 16), moved, packed)
            else:
                esend[...] = end[:, 0:16]
        if g == 2:
            osend[9] = packed
        waits.append(exchange(osend, orecv, first, last, send.at[4 + g], recv.at[4 + g], own.at[4 + g]))
        if g == 0:
            waits.append(exchange(esend, erecv, 0, 0, send.at[7], recv.at[7], own.at[7]))
    for _, sent in waits[:4]:
        sent()

    scale = float(NZL * SLABS) ** -0.5
    pieces = (
        (0, 24, 0, 192, -1.0, 0), (24, 48, 192, 0, 1.0, 0), (48, 72, 384, 384, 1.0, 0),
        (72, 96, 0, 192, -1.0, 1), (96, 120, 192, 0, 1.0, 1), (120, 128, 384, 384, 1.0, 1),
    )
    column = None
    for (first, last), wait in zip(groups, (4, 6, 7)):
        waits[wait][0]()
        for slot in range(first, min(last, 9)):
            lines = orecv[slot].T
            if slot == 0:
                column = lines
                continue
            k = slot - 1
            column = column + lines
            for low, high, at, to, sign, half in pieces:
                o1[half, pl.ds(at + k, high - low, stride=8), :] = lines[low:high]
                o2[half, pl.ds(to + k, high - low, stride=8), :] = column[low:high] * (sign * scale)
    waits[5][0]()
    ends = orecv[9].T
    end_column = erecv[...].T
    for k in range(NZL):
        end = ends[16 * k : 16 * k + 16]
        end_column = end_column + end
        o1[1, pl.ds(448 + k, 16, stride=8), :] = end
        o2[1, pl.ds(448 + k, 16, stride=8), :] = end_column * scale
    out = [
        pltpu.make_async_copy(src.at[half], dst.at[:, half * 128 : half * 128 + 128], loads.at[4 + 2 * i + half])
        for i, (src, dst) in enumerate(((o1, next_ref), (o2, pot_ref)))
        for half in range(2)
    ]
    for copy in out:
        copy.start()
    for _, sent in waits[4:]:
        sent()
    for copy in out:
        copy.wait()


def on_device(b_field, resist, ymix, zmix):
    flat = (3 * NX * NZL, NY)
    dma = pltpu.SemaphoreType.DMA
    b_next, potential = pl.pallas_call(
        kernel,
        name="step",
        out_shape=(jax.ShapeDtypeStruct(flat, F32), jax.ShapeDtypeStruct(flat, F32)),
        in_specs=[pl.BlockSpec(memory_space=pl.ANY)] * 4,
        out_specs=[pl.BlockSpec(memory_space=pl.ANY)] * 2,
        scratch_shapes=[
            pltpu.VMEM((4, NZL + 4, XR, NY), F32),
            pltpu.VMEM((3, NZL + 2, XR, NY), F32),
            pltpu.VMEM((LINES * 10, NY), F32),
            pltpu.VMEM((NY, NY), F32),
            pltpu.VMEM((8, 1024, 128), F32),
            pltpu.VMEM((1024, 128), F32),
            pltpu.VMEM((1152, 1024), BF16),
            pltpu.VMEM((1152, 1024), BF16),
            pltpu.VMEM((1024, 256), BF16),
            pltpu.VMEM((1024, 256), BF16),
            pltpu.VMEM((1152, 256), F32),
            pltpu.VMEM((8, SLABS, 128), F32),
            pltpu.VMEM((8, SLABS, 128), F32),
            pltpu.VMEM((2, SLABS, 64), F32),
            pltpu.VMEM((2, SLABS, 64), F32),
            pltpu.VMEM((10, SLABS, 128), F32),
            pltpu.VMEM((10, SLABS, 128), F32),
            pltpu.VMEM((SLABS, 16), F32),
            pltpu.VMEM((SLABS, 16), F32),
            pltpu.VMEM((2, flat[0], 128), F32),
            pltpu.VMEM((2, flat[0], 128), F32),
            dma((11,)), dma((11,)), dma((8,)), dma((8,)), dma((8,)), dma((8,)),
        ],
        compiler_params=pltpu.CompilerParams(
            collective_id=0, has_side_effects=True, vmem_limit_bytes=63 * 2**20
        ),
    )(b_field, resist, ymix, zmix)
    return b_next.reshape(b_field.shape), potential.reshape(b_field.shape)


def solution(mesh):
    in_specs = (P(None, "gx", "gz", None), P("gx", "gz", None), P(), P())
    out_specs = (P(None, "gx", "gz", None), P(None, "gx", "gz", None))
    return jax.shard_map(
        on_device, mesh=mesh, in_specs=in_specs, out_specs=out_specs, check_vma=False
    )
```

time: 66.4 us -> 62.5 us (0.941)
  the two profiles are of different devices: /device:TPU:8 before, /device:TPU:1 now
where the time goes in v1:
time: 62.5 us; the launch traced here: 62.3 us
  Pallas kernels  57.8 us (92%)
  local copies, waits for them, and re-layouts  3.83 us (6%)
  between operations  0.64 us (1%)
    pallas_call x1, Pallas kernels, on_device(): pl.pallas_call(kernel, name='step', out_shape=(jax.ShapeDtypeStruct(flat,...  57.8 us
    unnamed x2, local copies, waits for them, and re-layouts  3.83 us

profile of v1, /device:TPU:1, one launch (start us, length us, event | category | flops | bytes accessed | tf_op | source)
XLA Modules:
  0.0 62.3 jit_solution(2709995850747059187)
XLA Ops:
  0.6 57.8 %step.1 = (f32[576,256]{1,0:T(8,128)}, f32[576,256]{1,0:T(8,128)}) custom-call(f32[3,24,8,256]{3,2,1,0:T(8,128)} %b.1, f32[24,8,256]{2,1,0:T(8,128)} %res.1, f32[256,256]{1,0:T(8,128)} %ymix.1, f32[1024,1024]{1,0:T(8,128)} %zmix.1), custom_call_target="tpu_custom_call" | custom-call | tf_op jit(solution)/shard_map/step/pallas_call | solution.py:329
  58.5 1.9 %copy.8 = f32[3,24,8,256]{3,2,1,0:T(8,128)} copy(f32[3,24,8,256]{3,2,1,0:T(8,128)} %bitcast.3) | data formatting | bytes 1179648
  60.4 1.9 %copy.9 = f32[3,24,8,256]{3,2,1,0:T(8,128)} copy(f32[3,24,8,256]{3,2,1,0:T(8,128)} %bitcast.2) | data formatting | bytes 1179648

commit v2 on v1

v2 whole, which is shorter than its diff:
```python
import functools

import jax
import jax.numpy as jnp
from jax import lax
from jax.experimental import pallas as pl
from jax.experimental.pallas import tpu as pltpu
from jax.sharding import PartitionSpec as P

MESH = pl.DeviceIdType.MESH
F32, BF16 = jnp.float32, jnp.bfloat16
TIME_STEP = 0.1
NX, NZL, NY = 24, 8, 256
LINES = 3 * NX
SLABS = 128
XR = 32


def split(value):
    high = value.astype(BF16)
    return high, (value - high.astype(F32)).astype(BF16)


def dot(lhs, rhs, rhs_dim=0):
    return lax.dot_general(
        lhs, rhs, (((1,), (rhs_dim,)), ((), ())), preferred_element_type=F32
    )


def dot3(lhs, rhs, rhs_dim=0):
    (lhs_hi, lhs_lo), (rhs_hi, rhs_lo) = lhs, rhs
    small = dot(lhs_lo, rhs_hi, rhs_dim) + dot(lhs_hi, rhs_lo, rhs_dim)
    return small + dot(lhs_hi, rhs_hi, rhs_dim)


def diff(value, axis):
    size = value.shape[axis]
    return pltpu.roll(value, size - 1, axis) - pltpu.roll(value, 1, axis)


def halo_copies(b, res, bp, send, recv):
    gz, gx = lax.axis_index("gz"), lax.axis_index("gx")
    down, up = lax.rem(gz + SLABS - 1, SLABS), lax.rem(gz + 1, SLABS)
    other = 1 - gx
    near, far = (NX - 1) * other, gx + (NX - 2) * other
    near_row, far_row = 24 + 7 * other, 25 + 5 * other
    rows = slice(0, NX)
    same, cross = lambda z: {"gz": z}, lambda z: {"gz": z, "gx": other}
    plan = (
        (b.at[:, near], bp.at[0:3, 2:10, near_row], cross(gz)),
        (b.at[1:3, far], bp.at[1:3, 2:10, far_row], cross(gz)),
        (res.at[near], bp.at[3, 2:10, near_row], cross(gz)),
        (b.at[:, :, 0], bp.at[0:3, 10, rows], same(down)),
        (b.at[:, :, 7], bp.at[0:3, 1, rows], same(up)),
        (b.at[0:2, :, 1], bp.at[0:2, 11, rows], same(down)),
        (b.at[0:2, :, 6], bp.at[0:2, 0, rows], same(up)),
        (res.at[:, 0], bp.at[3, 10, rows], same(down)),
        (res.at[:, 7], bp.at[3, 1, rows], same(up)),
        (b.at[:, near, 0], bp.at[0:3, 10, near_row], cross(down)),
        (b.at[:, near, 7], bp.at[0:3, 1, near_row], cross(up)),
    )
    return [
        pltpu.make_async_remote_copy(
            src_ref=src,
            dst_ref=dst,
            send_sem=send.at[i],
            recv_sem=recv.at[i],
            device_id=where,
            device_id_type=MESH,
        )
        for i, (src, dst, where) in enumerate(plan)
    ]


def exchange(src, dst, spare, send, recv):
    me = lax.axis_index("gz")
    pltpu.make_async_copy(src.at[me], dst.at[me], recv).start()
    pltpu.make_async_copy(src.at[me], spare.at[0], send).start()

    @pl.loop(1, SLABS)
    def _(step):
        peer = lax.rem(me + step, SLABS)
        pltpu.make_async_remote_copy(
            src_ref=src.at[peer],
            dst_ref=dst.at[me],
            send_sem=send,
            recv_sem=recv,
            device_id={"gz": peer},
            device_id_type=MESH,
        ).start()

    def arrived():
        pltpu.make_async_copy(dst, dst, recv).wait()

    def sent():
        pltpu.make_async_copy(src, src, send).wait()

    return arrived, sent


def electric_plane(bp, ef, p):
    bx, by, bz, rs = bp[0, p], bp[1, p], bp[2, p], bp[3, p]
    jx = (diff(bz, 1) - (bp[1, p + 1] - bp[1, p - 1])) * 0.5
    jy = ((bp[0, p + 1] - bp[0, p - 1]) - diff(bz, 0)) * 0.5
    jz = (diff(by, 0) - diff(bx, 1)) * 0.5
    square = bx * bx + by * by + bz * bz
    inverse = 1.0 / (square + 1.0)
    along = (jx * bx + jy * by + jz * bz) * inverse
    factor = rs + square * inverse
    ef[0, p - 1] = jx * factor - bx * along
    ef[1, p - 1] = jy * factor - by * along
    ef[2, p - 1] = jz * factor - bz * along


def stepped_plane(bp, ef, st, r):
    ex, ey, ez = ef[0, r + 1], ef[1, r + 1], ef[2, r + 1]
    half = 0.5 * TIME_STEP
    cx = diff(ez, 1) - (ef[1, r + 2] - ef[1, r])
    cy = (ef[0, r + 2] - ef[0, r]) - diff(ez, 0)
    cz = diff(ey, 0) - diff(ex, 1)
    for c, curl in enumerate((cx, cy, cz)):
        row = pl.multiple_of(r * LINES + c * NX, 8)
        st[pl.ds(row, NX), :] = (bp[c, r + 2] - half * curl)[0:NX]


def mix_rows(rows, mixer, out, half):
    mixed = dot3(mixer, split(rows), 1)
    out[half] = mixed[0:SLABS]
    out[2 + half] = mixed[SLABS:]


def prepare(zv, zt, zhi, zlo, first, last):
    row_id = lax.broadcasted_iota(jnp.int32, (SLABS, SLABS), 0)
    col_id = lax.broadcasted_iota(jnp.int32, (SLABS, SLABS), 1)
    lower = (col_id < row_id).astype(F32)

    @pl.loop(first, last)
    def _(slot):
        r = lax.rem(slot + 2, NZL)
        for k in range(8):
            zt[k * 128 : (k + 1) * 128, :] = zv[k, pl.ds(r, SLABS, stride=8), :].T
        column = pl.ds(pl.multiple_of(slot * SLABS, SLABS), SLABS)
        total = jnp.zeros((SLABS, SLABS), F32)
        for k in range(8):
            part = zt[pl.ds(k, SLABS, stride=8), :]
            total = total + part
            zhi[k * 128 : (k + 1) * 128, column], zlo[k * 128 : (k + 1) * 128, column] = split(part)
        under = lax.dot_general(
            lower, total, (((1,), (0,)), ((), ())),
            precision=lax.Precision.HIGHEST, preferred_element_type=F32,
        )
        zhi[1024:1152, column], zlo[1024:1152, column] = split(under)


def take_rows(frecv, rhi, rlo, stream, half):
    lane = lax.broadcasted_iota(jnp.int32, (SLABS, 128), 1)
    got = frecv[2 * stream + half]
    got = jnp.concatenate([got, jnp.zeros((SLABS, 96), F32)], axis=1)
    for i in range(4):
        tile, off = divmod(i * LINES, 128)
        lines = got[:, tile * 128 : tile * 128 + 128]
        if off:
            lines = pltpu.roll(lines, 128 - off, 1)
        if off + LINES > 128:
            more = got[:, tile * 128 + 128 : tile * 128 + 256]
            lines = jnp.where(lane < 128 - off, lines, pltpu.roll(more, 128 - off, 1))
        row = (4 * half + i) * SLABS
        rhi[stream, row : row + SLABS, :], rlo[stream, row : row + SLABS, :] = split(lines)


def pack(pieces):
    lane = lax.broadcasted_iota(jnp.int32, (SLABS, 128), 1)
    tiles = {}
    for at, block in pieces:
        tile, off = divmod(at, 128)
        moved = pltpu.roll(block, off, 1) if off else block
        tiles[tile] = jnp.where(lane >= off, moved, tiles[tile]) if off else moved
        if off + LINES > 128:
            tiles[tile + 1] = moved
    return tiles


def mix_lines(zhi, zlo, rhi, rlo, osend, below, stream):
    pieces = []
    for first in range(0, 9, 3):
        rows = slice(first * SLABS, (first + 3) * SLABS)
        mixed = dot3((zhi[rows, :], zlo[rows, :]), (rhi[stream], rlo[stream]))
        for k in range(3):
            pieces.append(((first + k) * LINES, mixed[k * SLABS : (k + 1) * SLABS]))
    if stream == 0:
        below[...] = pieces.pop()[1]
    else:
        pieces[8:] = [(8 * LINES, below[...]), (9 * LINES, pieces[8][1])]
    for tile, value in pack(pieces).items():
        last = min(tile * 128 + 128, osend.shape[1])
        osend[:, tile * 128 : last] = value[:, 0 : last - tile * 128]


def kernel(
    b, res, ymix, zmix, ret0, ret1,
    bp, ef, st, yv, zv, zt, zhi, zlo, rhi, rlo, fsend, frecv, osend0, osend1, below,
    fspare, spare0, spare1, hs, hr, send, recv, loads,
):
    gz, gx = lax.axis_index("gz"), lax.axis_index("gx")
    load_b = [pltpu.make_async_copy(b.at[:, :, z], bp.at[0:3, z + 2, 0:NX], loads.at[0]) for z in range(NZL)]
    load_r = [pltpu.make_async_copy(res.at[:, z], bp.at[3, z + 2, 0:NX], loads.at[1]) for z in range(NZL)]
    load_y = pltpu.make_async_copy(ymix, yv, loads.at[2])
    load_z = [pltpu.make_async_copy(zmix.at[:, k * 128 : (k + 1) * 128], zv.at[k], loads.at[3]) for k in range(8)]
    for copy in (*load_b, *load_r, load_y, *load_z):
        copy.start()
    bp[:, :, NX:XR, :] = jnp.zeros((4, 12, XR - NX, NY), F32)

    barrier = pltpu.get_barrier_semaphore()
    other = 1 - gx
    down, up = lax.rem(gz + SLABS - 1, SLABS), lax.rem(gz + 1, SLABS)
    for z in (down, gz, up):
        pl.semaphore_signal(barrier, inc=1, device_id={"gz": z, "gx": other}, device_id_type=MESH)

    @pl.loop(1, SLABS)
    def _(step):
        peer = lax.rem(gz + step, SLABS)
        pl.semaphore_signal(barrier, inc=1, device_id={"gz": peer}, device_id_type=MESH)

    load_y.wait()
    mixer = split(yv[...].T)
    pl.semaphore_wait(barrier, SLABS + 2)
    halo = halo_copies(b, res, bp, hs, hr)
    for copy in halo:
        copy.start()

    pltpu.make_async_copy(bp.at[0:3, 2:10, 0:NX], bp.at[0:3, 2:10, 0:NX], loads.at[0]).wait()
    pltpu.make_async_copy(bp.at[3, 2:10, 0:NX], bp.at[3, 2:10, 0:NX], loads.at[1]).wait()
    for copy in halo[:3]:
        copy.wait()

    @pl.loop(3, 9)
    def _(p):
        electric_plane(bp, ef, p)

    @pl.loop(2, 6)
    def _(r):
        stepped_plane(bp, ef, st, r)

    mix_rows(st[2 * LINES : 6 * LINES, :], mixer, fsend, 0)
    waits = [exchange(fsend.at[0], frecv.at[0], fspare.at[0], send.at[0], recv.at[0])]
    for copy in halo[3:]:
        copy.wait()

    @pl.when(gz == 0)
    def _():
        bp[:, 0:2] = jnp.zeros((4, 2, XR, NY), F32)

    @pl.when(gz == SLABS - 1)
    def _():
        bp[:, 10:12] = jnp.zeros((4, 2, XR, NY), F32)

    for p in (1, 2, 9, 10):
        electric_plane(bp, ef, p)
    for r in (0, 1, 6, 7):
        stepped_plane(bp, ef, st, r)
    edges = jnp.concatenate([st[6 * LINES :, :], st[0 : 2 * LINES, :]], axis=0)
    mix_rows(edges, mixer, fsend, 1)
    for block in range(1, 4):
        waits.append(exchange(fsend.at[block], frecv.at[block], fspare.at[block], send.at[block], recv.at[block]))
    pltpu.make_async_copy(zv, zv, loads.at[3]).wait()
    prepare(zv, zt, zhi, zlo, 0, NZL)

    for stream, (osend, back, spare) in enumerate(((osend0, ret0, spare0), (osend1, ret1, spare1))):
        for half in range(2):
            waits[2 * stream + half][0]()
            take_rows(frecv, rhi, rlo, stream, half)
        mix_lines(zhi, zlo, rhi, rlo, osend, below, stream)
        waits.append(exchange(osend, back, spare, send.at[4 + stream], recv.at[4 + stream]))
    for _, sent in waits[:4]:
        sent()
    for arrived, sent in waits[4:]:
        arrived()
        sent()


def finish(ret0, ret1, next_ref, pot_ref, r0, r1, tv, o1, o2, loads):
    load = [pltpu.make_async_copy(ret0, r0, loads.at[0]), pltpu.make_async_copy(ret1, r1, loads.at[1])]
    for copy in load:
        copy.start()
    for stream, (copy, got) in enumerate(zip(load, (r0, r1))):
        copy.wait()
        width = got.shape[1]
        for at in range(0, width, 128):
            last = min(at + 128, width)
            tv[stream, at:last, :] = got[:, at:last].T

    scale = float(NZL * SLABS) ** -0.5
    out = []
    for stream in range(2):
        column = tv[1, (8 + stream) * LINES : (9 + stream) * LINES, :]
        for k in range(NZL):
            lines = tv[stream, k * LINES : (k + 1) * LINES, :]
            column = column + lines
            o1[stream, pl.ds(k, LINES, stride=8), :] = lines
            for at, to, sign in ((0, 192, -1.0), (24, 0, 1.0), (48, 384, 1.0)):
                o2[stream, pl.ds(to + k, NX, stride=8), :] = column[at : at + NX] * (sign * scale)
        for i, (src, dst) in enumerate(((o1, next_ref), (o2, pot_ref))):
            lanes = slice(stream * 128, stream * 128 + 128)
            out.append(pltpu.make_async_copy(src.at[stream], dst.at[:, lanes], loads.at[2 + 2 * stream + i]))
            out[-1].start()
    for copy in out:
        copy.wait()


def on_device(b_field, resist, ymix, zmix):
    flat = (3 * NX * NZL, NY)
    dma = pltpu.SemaphoreType.DMA
    anywhere = pl.BlockSpec(memory_space=pl.ANY)
    widths = (8 * LINES, 10 * LINES)
    returned = pl.pallas_call(
        kernel,
        name="step",
        out_shape=tuple(jax.ShapeDtypeStruct((SLABS, width), F32) for width in widths),
        in_specs=[anywhere] * 4,
        out_specs=[anywhere] * 2,
        scratch_shapes=[
            pltpu.VMEM((4, NZL + 4, XR, NY), F32),
            pltpu.VMEM((3, NZL + 2, XR, NY), F32),
            pltpu.VMEM((LINES * NZL, NY), F32),
            pltpu.VMEM((NY, NY), F32),
            pltpu.VMEM((8, 1024, 128), F32),
            pltpu.VMEM((1024, 128), F32),
            pltpu.VMEM((1152, 1024), BF16),
            pltpu.VMEM((1152, 1024), BF16),
            pltpu.VMEM((2, 1024, 128), BF16),
            pltpu.VMEM((2, 1024, 128), BF16),
            pltpu.VMEM((4, SLABS, 4 * LINES), F32),
            pltpu.VMEM((4, SLABS, 4 * LINES), F32),
            pltpu.VMEM((SLABS, widths[0]), F32),
            pltpu.VMEM((SLABS, widths[1]), F32),
            pltpu.VMEM((SLABS, 128), F32),
            pltpu.VMEM((4, 8, 4 * LINES), F32),
            pltpu.VMEM((8, widths[0]), F32),
            pltpu.VMEM((8, widths[1]), F32),
            dma((11,)), dma((11,)), dma((6,)), dma((6,)), dma((4,)),
        ],
        compiler_params=pltpu.CompilerParams(
            collective_id=0, has_side_effects=True, vmem_limit_bytes=63 * 2**20
        ),
    )(b_field, resist, ymix, zmix)
    b_next, potential = pl.pallas_call(
        finish,
        name="finish",
        out_shape=(jax.ShapeDtypeStruct(flat, F32), jax.ShapeDtypeStruct(flat, F32)),
        in_specs=[anywhere] * 2,
        out_specs=[anywhere] * 2,
        scratch_shapes=[
            pltpu.VMEM((SLABS, widths[0]), F32),
            pltpu.VMEM((SLABS, widths[1]), F32),
            pltpu.VMEM((2, widths[1], 128), F32),
            pltpu.VMEM((2, flat[0], 128), F32),
            pltpu.VMEM((2, flat[0], 128), F32),
            dma((6,)),
        ],
        compiler_params=pltpu.CompilerParams(vmem_limit_bytes=63 * 2**20),
    )(*returned)
    return b_next.reshape(b_field.shape), potential.reshape(b_field.shape)


def solution(mesh):
    in_specs = (P(None, "gx", "gz", None), P("gx", "gz", None), P(), P())
    out_specs = (P(None, "gx", "gz", None), P(None, "gx", "gz", None))
    return jax.shard_map(
        on_device, mesh=mesh, in_specs=in_specs, out_specs=out_specs, check_vma=False
    )
```

time: 62.5 us -> 56.2 us (0.90)
  local copies, waits for them, and re-layouts: 3.83 us -> 0 us
  Pallas kernels: 57.8 us -> 55.5 us
    unnamed x2 -> x0, local copies, waits for them, and re-layouts: 3.83 us -> none
    pallas_call x1 -> x2, Pallas kernels: 57.8 us -> 55.5 us  [the longest x1 53.1 us: on_device(): pl.pallas_call(kernel, name='step', out_shape=tuple((jax.ShapeDtypeStruct...]
where the time goes in v2:
time: 56.2 us; the launch traced here: 56.1 us
  Pallas kernels  55.5 us (99%)
  between operations  0.64 us (1%)
    pallas_call x1, Pallas kernels, on_device(): pl.pallas_call(kernel, name='step', out_shape=tuple((jax.ShapeDtypeStruct...  53.1 us
    pallas_call x1, Pallas kernels, on_device(): pl.pallas_call(finish, name='finish', out_shape=(jax.ShapeDtypeStruct(fla...  2.35 us

profile of v2, /device:TPU:1, one launch (start us, length us, event | category | flops | bytes accessed | tf_op | source)
XLA Modules:
  0.0 56.1 jit_solution(4072846829757449190)
XLA Ops:
  0.6 53.1 %step.1 = (f32[128,576]{1,0:T(8,128)}, f32[128,720]{1,0:T(8,128)}) custom-call(f32[3,24,8,256]{3,2,1,0:T(8,128)} %b.1, f32[24,8,256]{2,1,0:T(8,128)} %res.1, f32[256,256]{1,0:T(8,128)} %ymix.1, f32[1024,1024]{1,0:T(8,128)} %zmix.1), custom_call_target="tpu_custom_call" | custom-call | tf_op jit(solution)/shard_map/step/pallas_call | solution.py:315
  53.7 2.4 %finish.1 = (f32[576,256]{1,0:T(8,128)}, f32[576,256]{1,0:T(8,128)}) custom-call(f32[128,576]{1,0:T(8,128)} %get-tuple-element.6.ret0, f32[128,720]{1,0:T(8,128)} %get-tuple-element.7.ret1), custom_call_target="tpu_custom_call" | custom-call | tf_op jit(solution)/shard_map/finish/pallas_call | solution.py:346

commit v3 on v2

--- a/solution.py
+++ b/solution.py
@@ -38,7 +38,7 @@
     return pltpu.roll(value, size - 1, axis) - pltpu.roll(value, 1, axis)
 
 
-def halo_copies(b, res, bp, send, recv):
+def halo_copies(bp, send, recv):
     gz, gx = lax.axis_index("gz"), lax.axis_index("gx")
     down, up = lax.rem(gz + SLABS - 1, SLABS), lax.rem(gz + 1, SLABS)
     other = 1 - gx
@@ -47,17 +47,14 @@
     rows = slice(0, NX)
     same, cross = lambda z: {"gz": z}, lambda z: {"gz": z, "gx": other}
     plan = (
-        (b.at[:, near], bp.at[0:3, 2:10, near_row], cross(gz)),
-        (b.at[1:3, far], bp.at[1:3, 2:10, far_row], cross(gz)),
-        (res.at[near], bp.at[3, 2:10, near_row], cross(gz)),
-        (b.at[:, :, 0], bp.at[0:3, 10, rows], same(down)),
-        (b.at[:, :, 7], bp.at[0:3, 1, rows], same(up)),
-        (b.at[0:2, :, 1], bp.at[0:2, 11, rows], same(down)),
-        (b.at[0:2, :, 6], bp.at[0:2, 0, rows], same(up)),
-        (res.at[:, 0], bp.at[3, 10, rows], same(down)),
-        (res.at[:, 7], bp.at[3, 1, rows], same(up)),
-        (b.at[:, near, 0], bp.at[0:3, 10, near_row], cross(down)),
-        (b.at[:, near, 7], bp.at[0:3, 1, near_row], cross(up)),
+        (bp.at[:, 2:10, near], bp.at[:, 2:10, near_row], cross(gz)),
+        (bp.at[1:3, 2:10, far], bp.at[1:3, 2:10, far_row], cross(gz)),
+        (bp.at[:, 2, rows], bp.at[:, 10, rows], same(down)),
+        (bp.at[:, 9, rows], bp.at[:, 1, rows], same(up)),
+        (bp.at[0:3, 2, near], bp.at[0:3, 10, near_row], cross(down)),
+        (bp.at[0:3, 9, near], bp.at[0:3, 1, near_row], cross(up)),
+        (bp.at[0:2, 3, rows], bp.at[0:2, 11, rows], same(down)),
+        (bp.at[0:2, 8, rows], bp.at[0:2, 0, rows], same(up)),
     )
     return [
         pltpu.make_async_remote_copy(
@@ -72,14 +69,26 @@
     ]
 
 
+def each_peer(me, act):
+    for offsets in ((4,), (3, 5), (2, 6), (1, 7)):
+
+        @pl.loop(0, 16)
+        def _(step):
+            row = me + 8 * lax.rem(10 + 5 * step, 16)
+            for z in offsets:
+                act(lax.rem(row + z, SLABS))
+
+    @pl.loop(1, 16)
+    def _(step):
+        act(lax.rem(me + 8 * step, SLABS))
+
+
 def exchange(src, dst, spare, send, recv):
     me = lax.axis_index("gz")
     pltpu.make_async_copy(src.at[me], dst.at[me], recv).start()
     pltpu.make_async_copy(src.at[me], spare.at[0], send).start()
 
-    @pl.loop(1, SLABS)
-    def _(step):
-        peer = lax.rem(me + step, SLABS)
+    def push(peer):
         pltpu.make_async_remote_copy(
             src_ref=src.at[peer],
             dst_ref=dst.at[me],
@@ -88,6 +97,8 @@
             device_id={"gz": peer},
             device_id_type=MESH,
         ).start()
+
+    each_peer(me, push)
 
     def arrived():
         pltpu.make_async_copy(dst, dst, recv).wait()
@@ -202,35 +213,34 @@
     fspare, spare0, spare1, hs, hr, send, recv, loads,
 ):
     gz, gx = lax.axis_index("gz"), lax.axis_index("gx")
+    barrier = pltpu.get_barrier_semaphore()
+    other = 1 - gx
+    down, up = lax.rem(gz + SLABS - 1, SLABS), lax.rem(gz + 1, SLABS)
+
+    def ready(peer):
+        pl.semaphore_signal(barrier, inc=1, device_id={"gz": peer}, device_id_type=MESH)
+
+    each_peer(gz, ready)
+    bp[:, :, NX:XR, :] = jnp.zeros((4, 12, XR - NX, NY), F32)
+    for z in (down, gz, up):
+        pl.semaphore_signal(barrier, inc=1, device_id={"gz": z, "gx": other}, device_id_type=MESH)
+
     load_b = [pltpu.make_async_copy(b.at[:, :, z], bp.at[0:3, z + 2, 0:NX], loads.at[0]) for z in range(NZL)]
     load_r = [pltpu.make_async_copy(res.at[:, z], bp.at[3, z + 2, 0:NX], loads.at[1]) for z in range(NZL)]
     load_y = pltpu.make_async_copy(ymix, yv, loads.at[2])
     load_z = [pltpu.make_async_copy(zmix.at[:, k * 128 : (k + 1) * 128], zv.at[k], loads.at[3]) for k in range(8)]
     for copy in (*load_b, *load_r, load_y, *load_z):
         copy.start()
-    bp[:, :, NX:XR, :] = jnp.zeros((4, 12, XR - NX, NY), F32)
-
-    barrier = pltpu.get_barrier_semaphore()
-    other = 1 - gx
-    down, up = lax.rem(gz + SLABS - 1, SLABS), lax.rem(gz + 1, SLABS)
-    for z in (down, gz, up):
-        pl.semaphore_signal(barrier, inc=1, device_id={"gz": z, "gx": other}, device_id_type=MESH)
-
-    @pl.loop(1, SLABS)
-    def _(step):
-        peer = lax.rem(gz + step, SLABS)
-        pl.semaphore_signal(barrier, inc=1, device_id={"gz": peer}, device_id_type=MESH)
-
     load_y.wait()
     mixer = split(yv[...].T)
+    pltpu.make_async_copy(bp.at[0:3, 2:10, 0:NX], bp.at[0:3, 2:10, 0:NX], loads.at[0]).wait()
+    pltpu.make_async_copy(bp.at[3, 2:10, 0:NX], bp.at[3, 2:10, 0:NX], loads.at[1]).wait()
     pl.semaphore_wait(barrier, SLABS + 2)
-    halo = halo_copies(b, res, bp, hs, hr)
+    halo = halo_copies(bp, hs, hr)
     for copy in halo:
         copy.start()
 
-    pltpu.make_async_copy(bp.at[0:3, 2:10, 0:NX], bp.at[0:3, 2:10, 0:NX], loads.at[0]).wait()
-    pltpu.make_async_copy(bp.at[3, 2:10, 0:NX], bp.at[3, 2:10, 0:NX], loads.at[1]).wait()
-    for copy in halo[:3]:
+    for copy in halo[:2]:
         copy.wait()
 
     @pl.loop(3, 9)
@@ -243,7 +253,7 @@
 
     mix_rows(st[2 * LINES : 6 * LINES, :], mixer, fsend, 0)
     waits = [exchange(fsend.at[0], frecv.at[0], fspare.at[0], send.at[0], recv.at[0])]
-    for copy in halo[3:]:
+    for copy in halo[2:]:
         copy.wait()
 
     @pl.when(gz == 0)
@@ -337,7 +347,7 @@
             pltpu.VMEM((4, 8, 4 * LINES), F32),
             pltpu.VMEM((8, widths[0]), F32),
             pltpu.VMEM((8, widths[1]), F32),
-            dma((11,)), dma((11,)), dma((6,)), dma((6,)), dma((4,)),
+            dma((8,)), dma((8,)), dma((6,)), dma((6,)), dma((4,)),
         ],
         compiler_params=pltpu.CompilerParams(
             collective_id=0, has_side_effects=True, vmem_limit_bytes=63 * 2**20

time: 56.2 us -> 57.6 us (1.025)
  Pallas kernels: 55.5 us -> 56.8 us
    pallas_call x1, Pallas kernels: 53.1 us -> 54.5 us  [on_device(): pl.pallas_call(kernel, name='step', out_shape=tuple((jax.ShapeDtypeStruct...]
where the time goes in v3:
time: 57.6 us; the launch traced here: 57.5 us
  Pallas kernels  56.8 us (99%)
  between operations  0.64 us (1%)
    pallas_call x1, Pallas kernels, on_device(): pl.pallas_call(kernel, name='step', out_shape=tuple((jax.ShapeDtypeStruct...  54.5 us
    pallas_call x1, Pallas kernels, on_device(): pl.pallas_call(finish, name='finish', out_shape=(jax.ShapeDtypeStruct(fla...  2.35 us

profile of v3, /device:TPU:1, one launch (start us, length us, event | category | flops | bytes accessed | tf_op | source)
XLA Modules:
  0.0 57.5 jit_solution(16336502516378450762)
XLA Ops:
  0.6 54.5 %step.1 = (f32[128,576]{1,0:T(8,128)}, f32[128,720]{1,0:T(8,128)}) custom-call(f32[3,24,8,256]{3,2,1,0:T(8,128)} %b.1, f32[24,8,256]{2,1,0:T(8,128)} %res.1, f32[256,256]{1,0:T(8,128)} %ymix.1, f32[1024,1024]{1,0:T(8,128)} %zmix.1), custom_call_target="tpu_custom_call" | custom-call | tf_op jit(solution)/shard_map/step/pallas_call | solution.py:325
  55.1 2.4 %finish.1 = (f32[576,256]{1,0:T(8,128)}, f32[576,256]{1,0:T(8,128)}) custom-call(f32[128,576]{1,0:T(8,128)} %get-tuple-element.6.ret0, f32[128,720]{1,0:T(8,128)} %get-tuple-element.7.ret1), custom_call_target="tpu_custom_call" | custom-call | tf_op jit(solution)/shard_map/finish/pallas_call | solution.py:356

commit v4 on v3

--- a/solution.py
+++ b/solution.py
@@ -213,6 +213,10 @@
     fspare, spare0, spare1, hs, hr, send, recv, loads,
 ):
     gz, gx = lax.axis_index("gz"), lax.axis_index("gx")
+    load_b = [pltpu.make_async_copy(b.at[:, :, z], bp.at[0:3, z + 2, 0:NX], loads.at[0]) for z in range(NZL)]
+    load_r = [pltpu.make_async_copy(res.at[:, z], bp.at[3, z + 2, 0:NX], loads.at[1]) for z in range(NZL)]
+    for copy in (*load_b, *load_r):
+        copy.start()
     barrier = pltpu.get_barrier_semaphore()
     other = 1 - gx
     down, up = lax.rem(gz + SLABS - 1, SLABS), lax.rem(gz + 1, SLABS)
@@ -225,11 +229,9 @@
     for z in (down, gz, up):
         pl.semaphore_signal(barrier, inc=1, device_id={"gz": z, "gx": other}, device_id_type=MESH)
 
-    load_b = [pltpu.make_async_copy(b.at[:, :, z], bp.at[0:3, z + 2, 0:NX], loads.at[0]) for z in range(NZL)]
-    load_r = [pltpu.make_async_copy(res.at[:, z], bp.at[3, z + 2, 0:NX], loads.at[1]) for z in range(NZL)]
     load_y = pltpu.make_async_copy(ymix, yv, loads.at[2])
     load_z = [pltpu.make_async_copy(zmix.at[:, k * 128 : (k + 1) * 128], zv.at[k], loads.at[3]) for k in range(8)]
-    for copy in (*load_b, *load_r, load_y, *load_z):
+    for copy in (load_y, *load_z):
         copy.start()
     load_y.wait()
     mixer = split(yv[...].T)

time: 57.6 us -> 57.7 us (level)
  no operation moved by 1% of the time
where the time goes in v4:
time: 57.7 us; the launch traced here: 57.6 us
  Pallas kernels  57 us (99%)
  between operations  0.64 us (1%)
    pallas_call x1, Pallas kernels, on_device(): pl.pallas_call(kernel, name='step', out_shape=tuple((jax.ShapeDtypeStruct...  54.6 us
    pallas_call x1, Pallas kernels, on_device(): pl.pallas_call(finish, name='finish', out_shape=(jax.ShapeDtypeStruct(fla...  2.35 us

profile of v4, /device:TPU:1, one launch (start us, length us, event | category | flops | bytes accessed | tf_op | source)
XLA Modules:
  0.0 57.6 jit_solution(3442957573830007690)
XLA Ops:
  0.6 54.6 %step.1 = (f32[128,576]{1,0:T(8,128)}, f32[128,720]{1,0:T(8,128)}) custom-call(f32[3,24,8,256]{3,2,1,0:T(8,128)} %b.1, f32[24,8,256]{2,1,0:T(8,128)} %res.1, f32[256,256]{1,0:T(8,128)} %ymix.1, f32[1024,1024]{1,0:T(8,128)} %zmix.1), custom_call_target="tpu_custom_call" | custom-call | tf_op jit(solution)/shard_map/step/pallas_call | solution.py:327
  55.2 2.4 %finish.1 = (f32[576,256]{1,0:T(8,128)}, f32[576,256]{1,0:T(8,128)}) custom-call(f32[128,576]{1,0:T(8,128)} %get-tuple-element.6.ret0, f32[128,720]{1,0:T(8,128)} %get-tuple-element.7.ret1), custom_call_target="tpu_custom_call" | custom-call | tf_op jit(solution)/shard_map/finish/pallas_call | solution.py:358

commit v5 on v4

--- a/solution.py
+++ b/solution.py
@@ -69,26 +69,14 @@
     ]
 
 
-def each_peer(me, act):
-    for offsets in ((4,), (3, 5), (2, 6), (1, 7)):
-
-        @pl.loop(0, 16)
-        def _(step):
-            row = me + 8 * lax.rem(10 + 5 * step, 16)
-            for z in offsets:
-                act(lax.rem(row + z, SLABS))
-
-    @pl.loop(1, 16)
-    def _(step):
-        act(lax.rem(me + 8 * step, SLABS))
-
-
 def exchange(src, dst, spare, send, recv):
     me = lax.axis_index("gz")
     pltpu.make_async_copy(src.at[me], dst.at[me], recv).start()
     pltpu.make_async_copy(src.at[me], spare.at[0], send).start()
 
-    def push(peer):
+    @pl.loop(1, SLABS)
+    def _(step):
+        peer = lax.rem(me + step, SLABS)
         pltpu.make_async_remote_copy(
             src_ref=src.at[peer],
             dst_ref=dst.at[me],
@@ -97,8 +85,6 @@
             device_id={"gz": peer},
             device_id_type=MESH,
         ).start()
-
-    each_peer(me, push)
 
     def arrived():
         pltpu.make_async_copy(dst, dst, recv).wait()
@@ -215,24 +201,23 @@
     gz, gx = lax.axis_index("gz"), lax.axis_index("gx")
     load_b = [pltpu.make_async_copy(b.at[:, :, z], bp.at[0:3, z + 2, 0:NX], loads.at[0]) for z in range(NZL)]
     load_r = [pltpu.make_async_copy(res.at[:, z], bp.at[3, z + 2, 0:NX], loads.at[1]) for z in range(NZL)]
-    for copy in (*load_b, *load_r):
+    load_y = pltpu.make_async_copy(ymix, yv, loads.at[2])
+    load_z = [pltpu.make_async_copy(zmix.at[:, k * 128 : (k + 1) * 128], zv.at[k], loads.at[3]) for k in range(8)]
+    for copy in (*load_b, *load_r, load_y, *load_z):
         copy.start()
+    bp[:, :, NX:XR, :] = jnp.zeros((4, 12, XR - NX, NY), F32)
+
     barrier = pltpu.get_barrier_semaphore()
     other = 1 - gx
     down, up = lax.rem(gz + SLABS - 1, SLABS), lax.rem(gz + 1, SLABS)
-
-    def ready(peer):
-        pl.semaphore_signal(barrier, inc=1, device_id={"gz": peer}, device_id_type=MESH)
-
-    each_peer(gz, ready)
-    bp[:, :, NX:XR, :] = jnp.zeros((4, 12, XR - NX, NY), F32)
     for z in (down, gz, up):
         pl.semaphore_signal(barrier, inc=1, device_id={"gz": z, "gx": other}, device_id_type=MESH)
 
-    load_y = pltpu.make_async_copy(ymix, yv, loads.at[2])
-    load_z = [pltpu.make_async_copy(zmix.at[:, k * 128 : (k + 1) * 128], zv.at[k], loads.at[3]) for k in range(8)]
-    for copy in (load_y, *load_z):
-        copy.start()
+    @pl.loop(1, SLABS)
+    def _(step):
+        peer = lax.rem(gz + step, SLABS)
+        pl.semaphore_signal(barrier, inc=1, device_id={"gz": peer}, device_id_type=MESH)
+
     load_y.wait()
     mixer = split(yv[...].T)
     pltpu.make_async_copy(bp.at[0:3, 2:10, 0:NX], bp.at[0:3, 2:10, 0:NX], loads.at[0]).wait()

time: 57.7 us -> 56.1 us (0.972)
  the two profiles are of different devices: /device:TPU:1 before, /device:TPU:6 now
where the time goes in v5:
time: 56.1 us; the launch traced here: 56 us
  Pallas kernels  55.4 us (99%)
  between operations  0.64 us (1%)
    pallas_call x1, Pallas kernels, on_device(): pl.pallas_call(kernel, name='step', out_shape=tuple((jax.ShapeDtypeStruct...  53 us
    pallas_call x1, Pallas kernels, on_device(): pl.pallas_call(finish, name='finish', out_shape=(jax.ShapeDtypeStruct(fla...  2.35 us

profile of v5, /device:TPU:6, one launch (start us, length us, event | category | flops | bytes accessed | tf_op | source)
XLA Modules:
  0.0 56.0 jit_solution(708810600255341323)
XLA Ops:
  0.6 53.0 %step.1 = (f32[128,576]{1,0:T(8,128)}, f32[128,720]{1,0:T(8,128)}) custom-call(f32[3,24,8,256]{3,2,1,0:T(8,128)} %b.1, f32[24,8,256]{2,1,0:T(8,128)} %res.1, f32[256,256]{1,0:T(8,128)} %ymix.1, f32[1024,1024]{1,0:T(8,128)} %zmix.1), custom_call_target="tpu_custom_call" | custom-call | tf_op jit(solution)/shard_map/step/pallas_call | solution.py:312
  53.6 2.4 %finish.1 = (f32[576,256]{1,0:T(8,128)}, f32[576,256]{1,0:T(8,128)}) custom-call(f32[128,576]{1,0:T(8,128)} %get-tuple-element.6.ret0, f32[128,720]{1,0:T(8,128)} %get-tuple-element.7.ret1), custom_call_target="tpu_custom_call" | custom-call | tf_op jit(solution)/shard_map/finish/pallas_call | solution.py:343
